TPU v7x, 32 devices: a whole 2x2x4 slice. The times are simulated.
32 devices in a mesh: tm: 4 (over x, core), space: 8 (over z, y).
Axes of the slice: x: 2, y: 2, z: 4, core: 2. Of those that a mesh axis runs over, the one named last changes fastest.
Arguments:
- video_in: bfloat16 [16, 8, 16, 3072], P('tm', 'space'), may hold values from -6 to 6
- neighbours: int32 [8, 8], replicated, may hold values from 0 to 8, as said below
- valid_frames: int32 [8], replicated, may hold values from 0 to 16, as said below
- norm1_gain: float32 [192], replicated, may hold values from 0.1 to 1.9
- conv1_weight: bfloat16 [9, 576, 192], replicated, may hold values from -0.078125 to 0.078125
- conv1_bias: float32 [192], replicated, may hold values from -3 to 3
- norm2_gain: float32 [192], replicated, may hold values from 0.1 to 1.9
- conv2_weight: bfloat16 [9, 576, 192], replicated, may hold values from -0.078125 to 0.078125
- conv2_bias: float32 [192], replicated, may hold values from -3 to 3
Outputs:
- block_out: bfloat16 [16, 8, 16, 3072], P('tm', 'space')
Inputs may be any that keep to these rules, and one draw needn't show every extreme that they name: `neighbours`: entry k of a tile's row names the tile beside it in direction k of one placement of all tiles on a grid of 1 row by 8 columns, directions ordered (row, column) = (-1,-1), (-1,0), (-1,1), (0,-1), (0,1), (1,-1), (1,0), (1,1); 8 where that place lies outside the grid. `valid_frames`: frames from this number on are padding in that tile's track.
All inputs are finite; a program needn't handle non-finite values.
Results may differ from a plain program's by a relative error of at most 0.0037.
Values may be sent and summed in bfloat16 or wider, within the bound.
No kernel may reach another device: no remote copies, remote signals or barrier semaphores. Data moves between devices by JAX's collectives and lax.ppermute only.
A program may use at most 64 MiB of HBM per device.

v0:
```python
from functools import partial
import jax
import jax.numpy as jnp
from jax import lax
from jax.sharding import PartitionSpec as P

epsilon = 1e-06


def shifted(value, axis, steps):
    count = lax.axis_size(axis)
    first, last = (max(0, -steps), min(count, count - steps))
    return lax.ppermute(value, axis, [(source, source + steps) for source in range(first, last)])


def norm_silu(values, scale_gain):
    square = jnp.mean(values * values, axis=-1, keepdims=True)
    return jax.nn.silu(values * lax.rsqrt(square + epsilon) * scale_gain)


def conv_tile(framed, weight):
    frames_out = framed.shape[0] - 2
    side_len = framed.shape[1] - 2
    channels = framed.shape[-1]
    widened = jnp.concatenate(
        [framed[:, :, col_off : col_off + side_len] for col_off in range(3)], axis=-1
    )
    summed = jnp.zeros((frames_out * side_len * side_len, channels), jnp.float32)
    for time_off in range(3):
        for row_off in range(3):
            window = widened[
                time_off : time_off + frames_out, row_off : row_off + side_len
            ].reshape(-1, 3 * channels)
            summed = summed + jnp.dot(
                window, weight[time_off * 3 + row_off], preferred_element_type=jnp.float32
            )
    return summed.reshape(frames_out, side_len, side_len, channels)


def edge_pack(activation):
    return jnp.stack(
        [
            activation[:, :, -1],
            activation[:, :, :, -1],
            activation[:, :, :, 0],
            activation[:, :, 0],
        ],
        axis=2,
    )


def fold_edges(totals, portion, offset, nearby):
    amount = portion.shape[1]
    tile_ids = jnp.arange(amount, dtype=jnp.int32)
    choose = (nearby[:, :, None] == tile_ids[None, None, :]).astype(jnp.bfloat16)
    side_choose = jnp.stack([choose[:, 1], choose[:, 3], choose[:, 4], choose[:, 6]], axis=1)
    corner_choose = jnp.stack([choose[:, 0], choose[:, 2], choose[:, 5], choose[:, 7]], axis=1)
    corner_source = jnp.stack(
        [portion[:, :, 0, -1], portion[:, :, 0, 0], portion[:, :, 3, -1], portion[:, :, 3, 0]],
        axis=2,
    )
    new_sides = jnp.einsum(
        "djn,fnjxc->fdjxc", side_choose, portion, preferred_element_type=jnp.float32
    )
    new_corners = jnp.einsum(
        "djn,fnjc->fdjc", corner_choose, corner_source, preferred_element_type=jnp.float32
    )
    return (new_sides.astype(jnp.bfloat16), new_corners.astype(jnp.bfloat16))


def empty_rims(frame_count, activation):
    tiles_dev, side_len, channels = (activation.shape[1], activation.shape[2], activation.shape[4])
    return (
        jnp.zeros((frame_count, tiles_dev, 4, side_len, channels), jnp.bfloat16),
        jnp.zeros((frame_count, tiles_dev, 4, channels), jnp.bfloat16),
    )


def assemble(longer, side_rims, corners):
    top_row = jnp.concatenate([corners[:, :, 0:1], side_rims[:, :, 0], corners[:, :, 1:2]], axis=2)
    bottom_row = jnp.concatenate(
        [corners[:, :, 2:3], side_rims[:, :, 3], corners[:, :, 3:4]], axis=2
    )
    middle = jnp.concatenate(
        [side_rims[:, :, 1][:, :, :, None], longer, side_rims[:, :, 2][:, :, :, None]], axis=3
    )
    return jnp.concatenate([top_row[:, :, None], middle, bottom_row[:, :, None]], axis=2)


def extend(activation, nearby):
    frames_dev = activation.shape[0]
    folder = partial(fold_edges, nearby=nearby)
    side_rims, corners = folder(
        empty_rims(frames_dev, activation),
        lax.all_gather(edge_pack(activation), "space", axis=1, tiled=True),
        jnp.int32(0),
    )
    prev_act, prev_sides, prev_corners = shifted(
        (activation[frames_dev - 2 :], side_rims[frames_dev - 2 :], corners[frames_dev - 2 :]),
        "tm",
        1,
    )
    longer = jnp.concatenate([prev_act, activation], axis=0)
    side_rims = jnp.concatenate([prev_sides, side_rims], axis=0)
    corners = jnp.concatenate([prev_corners, corners], axis=0)
    return assemble(longer, side_rims, corners)


def blank_tile(pieces, tile_valid):
    framed = pieces[0]
    return jnp.zeros(
        (framed.shape[0] - 2, framed.shape[1] - 2, framed.shape[2] - 2, framed.shape[3]),
        jnp.bfloat16,
    )


def home_tiles(inputs, home_valid, first_frame, worker):
    pieces = tuple((stacked[:, 0] for stacked in inputs))
    results = [lax.cond(home_valid[0] > first_frame, worker, blank_tile, pieces, home_valid[0])]
    return jnp.stack(results, axis=1)


def on_device(
    video_in,
    neighbours,
    valid_frames,
    norm1_gain,
    conv1_weight,
    conv1_bias,
    norm2_gain,
    conv2_weight,
    conv2_bias,
):
    frames_dev, tiles_dev, side_len, merged = video_in.shape
    channels = norm1_gain.shape[0]
    voxels = video_in.reshape(frames_dev, tiles_dev, side_len, side_len, channels)
    first_frame = lax.axis_index("tm") * frames_dev
    home_ids = lax.axis_index("space") * tiles_dev + jnp.arange(tiles_dev, dtype=jnp.int32)
    home_valid = jnp.take(valid_frames, home_ids)
    nearby = jnp.take(neighbours, home_ids, axis=0)
    frame_pos = first_frame + jnp.arange(frames_dev, dtype=jnp.int32)
    present = (frame_pos[:, None] < home_valid[None, :]).astype(jnp.bfloat16)
    masked = voxels * present[:, :, None, None, None]
    activation = norm_silu(masked.astype(jnp.float32), norm1_gain).astype(jnp.bfloat16)

    def frame_weights(tile_valid):
        return (frame_pos < tile_valid).astype(jnp.float32)[:, None, None, None]

    def first_worker(pieces, tile_valid):
        summed = conv_tile(pieces[0], conv1_weight)
        return norm_silu((summed + conv1_bias) * frame_weights(tile_valid), norm2_gain).astype(
            jnp.bfloat16
        )

    def second_worker(pieces, tile_valid):
        summed = conv_tile(pieces[0], conv2_weight)
        return (
            (summed + conv2_bias) * frame_weights(tile_valid) + pieces[1].astype(jnp.float32)
        ).astype(jnp.bfloat16)

    padded = extend(activation, nearby)
    hidden = home_tiles((padded,), home_valid, first_frame, first_worker)
    padded = extend(hidden, nearby)
    block_out = home_tiles((padded, masked), home_valid, first_frame, second_worker)
    return block_out.reshape(frames_dev, tiles_dev, side_len, side_len * channels)


def solution(mesh):
    in_specs = (P("tm", "space", None, None), P(), P(), P(), P(), P(), P(), P(), P())
    out_specs = P("tm", "space", None, None)
    return jax.shard_map(
        on_device, mesh=mesh, in_specs=in_specs, out_specs=out_specs, check_vma=False
    )
```

profile of v0, /device:TPU:1, one launch (start us, length us, event | category | flops | bytes accessed | tf_op | source)
XLA Modules:
  0.0 148.6 jit_solution(2349354967583737358)
XLA Ops:
  0.0 1.6 %reshape.252 = bf16[4,1,16,16,192]{4,3,2,0,1:T(8,128)(2,1)S(1)} reshape(bf16[4,1,16,3072]{3,2,1,0:T(8,128)(2,1)} %param.13) | data formatting | bytes 786432 | tf_op jit(solution)/shard_map/reshape | solution.py:136
  1.6 1.2 dynamic-slice.5
  4.4 28.5 %all_gather.6 = bf16[4,8,4,16,192]{4,3,2,0,1:T(8,128)(2,1)S(1)} all-gather(bf16[4,1,4,16,192]{4,3,2,0,1:T(8,128)(2,1)S(1)} %pad_maximum_fusion.4), channel_id=1, replica_groups=mesh['tm'=4,'space'=8] {'space'}, dimensions={1}, use_global_device_ids=true | all-gather | bytes 884736 | tf_op jit(solution)/shard_map/all_gather | solution.py:95
  33.0 0.7 fusion.69
  34.0 9.1 %collective-permute-start = (bf16[2,1,4,192]{3,2,0,1:T(4,128)(2,1)S(1)}, bf16[2,1,4,192]{3,2,0,1:T(4,128)(2,1)S(1)}, u32[]{:S(2)}, u32[]{:S(2)}) collective-permute-start(bf16[2,1,4,192]{3,2,0,1:T(4,128)(2,1)S(1)} %slice.382), channel_id=1, source_target_pairs={{0,8},{8,16},{16,24},{1,9},{9,17},{17,25},{2,10},{10,18},{18,26},{... | collective-permute-start | bytes 9224 | tf_op jit(solution)/shard_map/ppermute | solution.py:13
  43.2 0.7 fusion.12
  43.9 1.9 %collective-permute-start.1 = (bf16[2,1,4,16,192]{4,3,0,2,1:T(8,128)(2,1)S(1)}, bf16[2,1,4,16,192]{4,3,0,2,1:T(8,128)(2,1)S(1)}, u32[]{:S(2)}, u32[]{:S(2)}) collective-permute-start(bf16[2,1,4,16,192]{4,3,0,2,1:T(8,128)(2,1)S(1)} %slice.385), channel_id=1, source_target_pairs={{0,8},{8,16},{16,24},{1,9},{9,17},{17,25},{2,10},{10,18},{18,26},{... | collective-permute-start | bytes 147464 | tf_op jit(solution)/shard_map/ppermute | solution.py:13
  45.9 1.9 %collective-permute-start.2 = (bf16[2,1,16,16,192]{4,3,2,0,1:T(8,128)(2,1)S(1)}, bf16[2,1,16,16,192]{4,3,2,0,1:T(8,128)(2,1)S(1)}, u32[]{:S(2)}, u32[]{:S(2)}) collective-permute-start(bf16[2,1,16,16,192]{4,3,2,0,1:T(8,128)(2,1)S(1)} %slice.392), channel_id=1, source_target_pairs={{0,8},{8,16},{16,24},{1,9},{9,17},{17,25},{2,10},{10,18},{18,26},{... | collective-permute-start | bytes 589832 | tf_op jit(solution)/shard_map/ppermute | solution.py:13
  48.2 2.9 %collective-permute-done.2 = bf16[2,1,16,16,192]{4,3,2,0,1:T(8,128)(2,1)S(1)} collective-permute-done((bf16[2,1,16,16,192]{4,3,2,0,1:T(8,128)(2,1)S(1)}, bf16[2,1,16,16,192]{4,3,2,0,1:T(8,128)(2,1)S(1)}, u32[]{:S(2)}, u32[]{:S(2)}) %collective-permute-start.2) | collective-permute-done | bytes 196640 | tf_op jit(solution)/shard_map/ppermute | solution.py:13
  51.1 0.9 pad_maximum_fusion.2
  52.0 24.7 %conditional.2 = (bf16[4,16,16,192]{3,2,1,0:T(8,128)(2,1)S(1)}) conditional(s32[]{:T(128)} %convert_element_type.107, () %tuple.20, (bf16[6,1,18,18,192]{4,3,2,0,1:T(8,128)(2,1)S(1)}, bf16[9,576,192]{1,2,0:T(8,128)(2,1)}, f32[192]{0:T(256)S(1)}, s32[]{:T(128)}, s32[4]{0:T(128)S(1)}, /*index=5*/f32[192]{0:T(256)S(1)}) %tuple.102), branch_computations={%region_1.2_spmd, %region_2.4_spmd} | conditional | flops 2048533504 | bytes 96561936 | solution.py:119
  52.0 0.7 fusion.73
  52.7 0.9 pad_maximum_fusion
  53.6 4.4 %fusion.72 = (bf16[4,16,16,576]{3,2,1,0:T(8,128)(2,1)}, bf16[4,16,16,576]{3,2,1,0:T(8,128)(2,1)}, bf16[4,16,16,576]{3,2,1,0:T(8,128)(2,1)}, bf16[4,16,16,576]{3,...) fusion(bf16[6,18,16,576]{3,2,1,0:T(8,128)(2,1)S(1)} %pad_maximu, ...), kind=kLoop, calls=%fused_computation.174 | loop fusion | bytes 21233664 | tf_op jit(solution)/shard_map/cond/branch_1_fun/slice | solution.py:31
  58.0 4.1 %copy.179 = bf16[9,576,192]{2,1,0:T(8,128)(2,1)S(1)} copy(bf16[9,576,192]{1,2,0:T(8,128)(2,1)} %get-tuple-element.168) | data formatting | bytes 3981312 | tf_op jit(solution)/shard_map
  62.1 2.0 %fusion = f32[1024,192]{0,1:T(8,128)S(1)} fusion(bf16[1024,576]{1,0:T(8,128)(2,1)} %bitcast.249, bf16[9,576,192]{2,1,0:T(8,128)(2,1)S(1)} %copy.179), kind=kOutput, calls=%fused_computation.20 | convolution fusion | flops 226492416 | bytes 2260992 | tf_op jit(solution)/shard_map/cond/branch_1_fun/dot_general | solution.py:34
  64.8 0.7 copy-done.11
  66.1 0.7 copy-done.9
  67.4 0.7 copy-done.7
  68.7 0.7 copy-done.5
  70.1 0.7 copy-done.3
  71.4 0.7 copy-done.1
  72.1 1.5 %convolution_add_fusion.1 = f32[1024,192]{0,1:T(8,128)} fusion(f32[1024,192]{0,1:T(8,128)S(1)} %convolution_add_fusion.2, bf16[1024,576]{1,0:T(8,128)(2,1)S(1)} %bitcast.235, bf16[9,576,192]{2,1,0:T(8,128)(2,1)S(1)} %copy.179), kind=kOutput, calls=%fused_computation.2 | convolution fusion | flops 226689024 | bytes 3178496 | tf_op jit(solution)/shard_map/cond/branch_1_fun/dot_general | solution.py:34
  73.7 2.2 %multiply_reduce_fusion = (f32[1024]{0:T(1024)S(1)}, f32[1024,192]{0,1:T(8,128)S(1)}) fusion(f32[1024]{0:T(1024)S(1)} %mul.124, f32[192]{0:T(256)S(1)} %get-tuple-element.60, f32[1024,192]{0,1:T(8,128)} %convolution_add_fusion.1, bf16[1024,576]{1,0:T(8,128)(2,1)} %bitcast.233, bf16[9,576,192]{2,1,0:T(8,128)(2,1)S(1)} %copy.179), kind=kOutput, calls=%fused_computation.10 | convolution fusion | flops 227474432 | bytes 3056640 | tf_op jit(solution)/shard_map/cond/branch_1_fun/dot_general | solution.py:34
  77.0 29.7 %all_gather.7 = bf16[4,8,4,16,192]{4,3,2,0,1:T(8,128)(2,1)S(1)} all-gather(bf16[4,1,4,16,192]{4,3,2,0,1:T(8,128)(2,1)S(1)} %pad_maximum_fusion.5), channel_id=1, replica_groups=mesh['tm'=4,'space'=8] {'space'}, dimensions={1}, use_global_device_ids=true | all-gather | bytes 884736 | tf_op jit(solution)/shard_map/all_gather | solution.py:95
  106.8 0.7 fusion.10
  107.8 8.5 %collective-permute-start.3 = (bf16[2,1,4,192]{3,2,0,1:T(4,128)(2,1)S(1)}, bf16[2,1,4,192]{3,2,0,1:T(4,128)(2,1)S(1)}, u32[]{:S(2)}, u32[]{:S(2)}) collective-permute-start(bf16[2,1,4,192]{3,2,0,1:T(4,128)(2,1)S(1)} %slice.405), channel_id=1, source_target_pairs={{0,8},{8,16},{16,24},{1,9},{9,17},{17,25},{2,10},{10,18},{18,26},{... | collective-permute-start | bytes 9224 | tf_op jit(solution)/shard_map/ppermute | solution.py:13
  116.3 1.9 %collective-permute-start.4 = (bf16[2,1,4,16,192]{4,3,0,2,1:T(8,128)(2,1)S(1)}, bf16[2,1,4,16,192]{4,3,0,2,1:T(8,128)(2,1)S(1)}, u32[]{:S(2)}, u32[]{:S(2)}) collective-permute-start(bf16[2,1,4,16,192]{4,3,0,2,1:T(8,128)(2,1)S(1)} %slice.408), channel_id=1, source_target_pairs={{0,8},{8,16},{16,24},{1,9},{9,17},{17,25},{2,10},{10,18},{18,26},{... | collective-permute-start | bytes 147464 | tf_op jit(solution)/shard_map/ppermute | solution.py:13
  118.2 1.9 %collective-permute-start.5 = (bf16[2,1,16,16,192]{4,3,2,0,1:T(8,128)(2,1)S(1)}, bf16[2,1,16,16,192]{4,3,2,0,1:T(8,128)(2,1)S(1)}, u32[]{:S(2)}, u32[]{:S(2)}) collective-permute-start(bf16[2,1,16,16,192]{4,3,2,0,1:T(8,128)(2,1)S(1)} %slice_bitcast_fusion.36), channel_id=1, source_target_pairs={{0,8},{8,16},{16,24},{1,9},{9,17},{17,25},{2,10},{10,18},{18,26},{... | collective-permute-start | bytes 589832 | tf_op jit(solution)/shard_map/ppermute | solution.py:13
  120.5 2.9 %collective-permute-done.5 = bf16[2,1,16,16,192]{4,3,2,0,1:T(8,128)(2,1)S(1)} collective-permute-done((bf16[2,1,16,16,192]{4,3,2,0,1:T(8,128)(2,1)S(1)}, bf16[2,1,16,16,192]{4,3,2,0,1:T(8,128)(2,1)S(1)}, u32[]{:S(2)}, u32[]{:S(2)}) %collective-permute-start.5) | collective-permute-done | bytes 196640 | tf_op jit(solution)/shard_map/ppermute | solution.py:13
  123.5 0.9 pad_maximum_fusion.3
  124.3 24.3 %conditional.3 = (bf16[4,1,16,3072]{3,2,0,1:T(8,128)(2,1)}) conditional(s32[]{:T(128)} %convert_element_type.107, () %tuple.19, (bf16[6,1,18,18,192]{4,3,2,0,1:T(8,128)(2,1)S(1)}, bf16[9,576,192]{1,2,0:T(8,128)(2,1)}, f32[192]{0:T(256)S(1)}, s32[]{:T(128)}, s32[4]{0:T(128)S(1)}, /*index=5*/bf16[4]{0:T(256)(128)(2,1)S(1)}, ...), branch_computations={%region_4.5_spmd, %region_5.6_spmd} | conditional | flops 2047156224 | bytes 104957008 | solution.py:119
  124.4 0.7 fusion.75
  125.1 0.9 pad_maximum_fusion.1
  125.9 4.4 %fusion.74 = (bf16[4,16,16,576]{3,2,1,0:T(8,128)(2,1)}, bf16[4,16,16,576]{3,2,1,0:T(8,128)(2,1)}, bf16[4,16,16,576]{3,2,1,0:T(8,128)(2,1)}, bf16[4,16,16,576]{3,...) fusion(bf16[6,18,16,576]{3,2,1,0:T(8,128)(2,1)S(1)} %pad_maximu, ...), kind=kLoop, calls=%fused_computation.176 | loop fusion | bytes 21233664 | tf_op jit(solution)/shard_map/cond/branch_1_fun/slice | solution.py:31
  130.3 4.1 %copy.190 = bf16[9,576,192]{2,1,0:T(8,128)(2,1)S(1)} copy(bf16[9,576,192]{1,2,0:T(8,128)(2,1)} %get-tuple-element.174) | data formatting | bytes 3981312 | tf_op jit(solution)/shard_map
  134.4 2.0 %fusion.1 = f32[1024,192]{0,1:T(8,128)S(1)} fusion(bf16[1024,576]{1,0:T(8,128)(2,1)} %bitcast.250, bf16[9,576,192]{2,1,0:T(8,128)(2,1)S(1)} %copy.190), kind=kOutput, calls=%fused_computation.43 | convolution fusion | flops 226492416 | bytes 2260992 | tf_op jit(solution)/shard_map/cond/branch_1_fun/dot_general | solution.py:34
  136.5 0.6 convolution_add_fusion.15
  137.1 0.7 copy-done.12
  137.8 0.6 convolution_add_fusion.14
  138.4 0.7 copy-done.10
  139.7 0.7 copy-done.8
  141.1 0.7 copy-done.6
  142.4 0.7 copy-done.4
  143.7 0.7 copy-done.2
  145.0 0.7 copy-done
  145.7 0.6 convolution_add_fusion.8
  147.7 0.9 add_convert_fusion
  (107 shorter events, 11.6 us)
Async XLA Ops:
  0.0 3.7 %copy-start.17 = (f32[192]{0:T(256)S(1)}, f32[192]{0:T(256)}, u32[]{:S(2)}) copy-start(f32[192]{0:T(256)} %param.16) | copy-start | bytes 2308
  34.0 13.8 %collective-permute-start = (bf16[2,1,4,192]{3,2,0,1:T(4,128)(2,1)S(1)}, bf16[2,1,4,192]{3,2,0,1:T(4,128)(2,1)S(1)}, u32[]{:S(2)}, u32[]{:S(2)}) collective-permute-start(bf16[2,1,4,192]{3,2,0,1:T(4,128)(2,1)S(1)} %slice.382), channel_id=1, source_target_pairs={{0,8},{8,16},{16,24},{1,9},{9,17},{17,25},{2,10},{10,18},{18,26},{... | collective-permute-start | bytes 9224 | tf_op jit(solution)/shard_map/ppermute | solution.py:13
  43.9 4.0 %collective-permute-start.1 = (bf16[2,1,4,16,192]{4,3,0,2,1:T(8,128)(2,1)S(1)}, bf16[2,1,4,16,192]{4,3,0,2,1:T(8,128)(2,1)S(1)}, u32[]{:S(2)}, u32[]{:S(2)}) collective-permute-start(bf16[2,1,4,16,192]{4,3,0,2,1:T(8,128)(2,1)S(1)} %slice.385), channel_id=1, source_target_pairs={{0,8},{8,16},{16,24},{1,9},{9,17},{17,25},{2,10},{10,18},{18,26},{... | collective-permute-start | bytes 147464 | tf_op jit(solution)/shard_map/ppermute | solution.py:13
  45.9 5.2 %collective-permute-start.2 = (bf16[2,1,16,16,192]{4,3,2,0,1:T(8,128)(2,1)S(1)}, bf16[2,1,16,16,192]{4,3,2,0,1:T(8,128)(2,1)S(1)}, u32[]{:S(2)}, u32[]{:S(2)}) collective-permute-start(bf16[2,1,16,16,192]{4,3,2,0,1:T(8,128)(2,1)S(1)} %slice.392), channel_id=1, source_target_pairs={{0,8},{8,16},{16,24},{1,9},{9,17},{17,25},{2,10},{10,18},{18,26},{... | collective-permute-start | bytes 589832 | tf_op jit(solution)/shard_map/ppermute | solution.py:13
  48.2 3.8 %copy-start.16 = (f32[192]{0:T(256)S(1)}, f32[192]{0:T(256)}, u32[]{:S(2)}) copy-start(f32[192]{0:T(256)} %param.18) | copy-start | bytes 2308
  48.2 3.8 %copy-start.19 = (f32[192]{0:T(256)S(1)}, f32[192]{0:T(256)}, u32[]{:S(2)}) copy-start(f32[192]{0:T(256)} %param.19) | copy-start | bytes 2308
  62.1 2.0 %copy-start.13 = (bf16[4,16,16,576]{3,2,1,0:T(8,128)(2,1)S(1)}, bf16[4,16,16,576]{3,2,1,0:T(8,128)(2,1)}, u32[]{:S(2)}) copy-start(bf16[4,16,16,576]{3,2,1,0:T(8,128)(2,1)} %get-tuple-element.187) | copy-start | bytes 3538948 | tf_op jit(solution)/shard_map/cond
  64.2 1.3 copy-start.11
  65.5 1.3 copy-start.9
  66.8 1.3 copy-start.7
  68.1 1.3 copy-start.5
  69.4 1.3 copy-start.3
  70.7 1.3 copy-start.1
  107.8 12.4 %collective-permute-start.3 = (bf16[2,1,4,192]{3,2,0,1:T(4,128)(2,1)S(1)}, bf16[2,1,4,192]{3,2,0,1:T(4,128)(2,1)S(1)}, u32[]{:S(2)}, u32[]{:S(2)}) collective-permute-start(bf16[2,1,4,192]{3,2,0,1:T(4,128)(2,1)S(1)} %slice.405), channel_id=1, source_target_pairs={{0,8},{8,16},{16,24},{1,9},{9,17},{17,25},{2,10},{10,18},{18,26},{... | collective-permute-start | bytes 9224 | tf_op jit(solution)/shard_map/ppermute | solution.py:13
  116.3 3.9 %collective-permute-start.4 = (bf16[2,1,4,16,192]{4,3,0,2,1:T(8,128)(2,1)S(1)}, bf16[2,1,4,16,192]{4,3,0,2,1:T(8,128)(2,1)S(1)}, u32[]{:S(2)}, u32[]{:S(2)}) collective-permute-start(bf16[2,1,4,16,192]{4,3,0,2,1:T(8,128)(2,1)S(1)} %slice.408), channel_id=1, source_target_pairs={{0,8},{8,16},{16,24},{1,9},{9,17},{17,25},{2,10},{10,18},{18,26},{... | collective-permute-start | bytes 147464 | tf_op jit(solution)/shard_map/ppermute | solution.py:13
  118.2 5.2 %collective-permute-start.5 = (bf16[2,1,16,16,192]{4,3,2,0,1:T(8,128)(2,1)S(1)}, bf16[2,1,16,16,192]{4,3,2,0,1:T(8,128)(2,1)S(1)}, u32[]{:S(2)}, u32[]{:S(2)}) collective-permute-start(bf16[2,1,16,16,192]{4,3,2,0,1:T(8,128)(2,1)S(1)} %slice_bitcast_fusion.36), channel_id=1, source_target_pairs={{0,8},{8,16},{16,24},{1,9},{9,17},{17,25},{2,10},{10,18},{18,26},{... | collective-permute-start | bytes 589832 | tf_op jit(solution)/shard_map/ppermute | solution.py:13
  120.5 3.9 %copy-start.18 = (f32[192]{0:T(256)S(1)}, f32[192]{0:T(256)}, u32[]{:S(2)}) copy-start(f32[192]{0:T(256)} %param.21) | copy-start | bytes 2308
  134.4 2.0 %copy-start.14 = (bf16[4,16,16,576]{3,2,1,0:T(8,128)(2,1)S(1)}, bf16[4,16,16,576]{3,2,1,0:T(8,128)(2,1)}, u32[]{:S(2)}) copy-start(bf16[4,16,16,576]{3,2,1,0:T(8,128)(2,1)} %get-tuple-element.201) | copy-start | bytes 3538948 | tf_op jit(solution)/shard_map/cond
  136.5 1.3 copy-start.12
  137.8 1.3 copy-start.10
  139.1 1.3 copy-start.8
  140.4 1.3 copy-start.6
  141.7 1.3 copy-start.4
  143.1 1.3 copy-start.2
  144.4 1.3 copy-start
  146.7 1.0 copy-start.15
where the time goes:
time: 150 us; the launch traced here: 149 us
  blocking collectives  58.2 us (39%)
  local copies, waits for them, and re-layouts  33 us (22%)
  starting transfers between devices  25.3 us (17%)
  matrix products  18.2 us (12%)
  other arithmetic  6.69 us (4%)
  waiting for transfers between devices  5.81 us (4%)
    all_gather x2, blocking collectives, extend(): lax.all_gather(edge_pack(activation), 'space', axis=1, tiled=True)  58.2 us
    ppermute x6, starting transfers between devices, shifted(): lax.ppermute(value, axis, [(source, source + steps) for source in range(f...  25.3 us
    dot_general x18, matrix products, conv_tile(): jnp.dot(window, weight[time_off * 3 + row_off], preferred_element_type=jn...  16.4 us
    cond x32, local copies, waits for them, and re-layouts  9.47 us
    slice x2, local copies, waits for them, and re-layouts, conv_tile(): widened[time_off:time_off + frames_out, row_off:row_off + side_len]  8.86 us
    another operation x2, local copies, waits for them, and re-layouts  8.17 us
    ppermute x6, waiting for transfers between devices, shifted(): lax.ppermute(value, axis, [(source, source + steps) for source in range(f...  5.81 us
  transfers between devices with their start and end apart: 6, of which 2 were waited for; matrix products, arithmetic and copies ran while one was open for 1% of the time, Pallas kernels for 0%

commit v1 on v0

--- a/solution.py
+++ b/solution.py
@@ -5,6 +5,19 @@
 from jax.sharding import PartitionSpec as P
 
 epsilon = 1e-06
+
+
+def collect(x, axis, dim):
+    ways = lax.axis_size(axis)
+    up = [(d, (d + 1) % ways) for d in range(ways)]
+    down = [(d, (d - 1) % ways) for d in range(ways)]
+    earlier, later = ([x], [x])
+    for _ in range(ways // 2):
+        earlier.append(lax.ppermute(earlier[-1], axis, up))
+    for _ in range((ways - 1) // 2):
+        later.append(lax.ppermute(later[-1], axis, down))
+    line = jnp.concatenate([*earlier[::-1], *later[1:]], axis=dim)
+    return jnp.roll(line, (lax.axis_index(axis) - ways // 2) * x.shape[dim], axis=dim)
 
 
 def shifted(value, axis, steps):
@@ -91,9 +104,7 @@
     frames_dev = activation.shape[0]
     folder = partial(fold_edges, nearby=nearby)
     side_rims, corners = folder(
-        empty_rims(frames_dev, activation),
-        lax.all_gather(edge_pack(activation), "space", axis=1, tiled=True),
-        jnp.int32(0),
+        empty_rims(frames_dev, activation), collect(edge_pack(activation), "space", 1), jnp.int32(0)
     )
     prev_act, prev_sides, prev_corners = shifted(
         (activation[frames_dev - 2 :], side_rims[frames_dev - 2 :], corners[frames_dev - 2 :]),

time: 150 us -> 141 us (0.940)
  blocking collectives: 58.2 us -> 0 us
  waiting for transfers between devices: 5.81 us -> 30.3 us
  starting transfers between devices: 25.3 us -> 48.1 us
    all_gather x2 -> x0, blocking collectives: 58.2 us -> none  [extend(): lax.all_gather(edge_pack(activation), 'space', axis=1, tiled=True)]
    ppermute x0 -> x14, starting transfers between devices: none -> 28.6 us  [the longest x6 23.8 us: collect(): later.append(lax.ppermute(later[-1], axis, down))]
    ppermute x0 -> x14, waiting for transfers between devices: none -> 27.8 us  [the longest x8 26 us: collect(): earlier.append(lax.ppermute(earlier[-1], axis, up))]
    ppermute x6, starting transfers between devices: 25.3 us -> 19.5 us  [shifted(): lax.ppermute(value, axis, [(source, source + steps) for source in range(f...]
    ppermute x6, waiting for transfers between devices: 5.81 us -> 2.53 us  [shifted(): lax.ppermute(value, axis, [(source, source + steps) for source in range(f...]
  transfers between devices with their start and end apart: 6 -> 20, of which waited for: 2 -> 9; matrix products, arithmetic and copies ran while one was open for 1% -> 3% of each run, Pallas kernels for 0% -> 0%
where the time goes in v1:
time: 141 us; the launch traced here: 139 us
  starting transfers between devices  48.1 us (34%)
  local copies, waits for them, and re-layouts  33.2 us (24%)
  waiting for transfers between devices  30.3 us (21%)
  matrix products  18.2 us (13%)
  other arithmetic  7.65 us (5%)
    ppermute x8, waiting for transfers between devices, collect(): earlier.append(lax.ppermute(earlier[-1], axis, up))  26 us
    ppermute x6, starting transfers between devices, collect(): later.append(lax.ppermute(later[-1], axis, down))  23.8 us
    ppermute x6, starting transfers between devices, shifted(): lax.ppermute(value, axis, [(source, source + steps) for source in range(f...  19.5 us
    dot_general x18, matrix products, conv_tile(): jnp.dot(window, weight[time_off * 3 + row_off], preferred_element_type=jn...  16.4 us
    cond x32, local copies, waits for them, and re-layouts  9.47 us
    slice x2, local copies, waits for them, and re-layouts, conv_tile(): widened[time_off:time_off + frames_out, row_off:row_off + side_len]  8.82 us
    another operation x2, local copies, waits for them, and re-layouts  8.17 us
    ppermute x8, starting transfers between devices, collect(): earlier.append(lax.ppermute(earlier[-1], axis, up))  4.78 us
  transfers between devices with their start and end apart: 20, of which 9 were waited for; matrix products, arithmetic and copies ran while one was open for 3% of the time, Pallas kernels for 0%

profile of v1, /device:TPU:1, one launch (start us, length us, event | category | flops | bytes accessed | tf_op | source)
XLA Modules:
  0.0 139.4 jit_solution(15550627138121118230)
XLA Ops:
  0.0 1.6 %reshape.252 = bf16[4,1,16,16,192]{4,3,2,0,1:T(8,128)(2,1)S(1)} reshape(bf16[4,1,16,3072]{3,2,1,0:T(8,128)(2,1)} %param.15) | data formatting | bytes 786432 | tf_op jit(solution)/shard_map/reshape | solution.py:147
  1.6 1.2 dynamic-slice.5
  4.3 2.1 %collective-permute-start = (bf16[4,1,4,16,192]{4,3,2,0,1:T(8,128)(2,1)S(1)}, bf16[4,1,4,16,192]{4,3,2,0,1:T(8,128)(2,1)S(1)}, u32[]{:S(2)}, u32[]{:S(2)}) collective-permute-start(bf16[4,1,4,16,192]{4,3,2,0,1:T(8,128)(2,1)S(1)} %pad_maximum_fusion.4), channel_id=1, source_target_pairs={{0,1},{1,2},{2,3},{3,4},{4,5},{5,6},{6,7},{7,0},{8,9},{9,10},{10,1... | collective-permute-start | bytes 294920 | tf_op jit(solution)/shard_map/ppermute | solution.py:16
  6.5 3.1 %collective-permute-start.4 = (bf16[4,1,4,16,192]{4,3,2,0,1:T(8,128)(2,1)S(1)}, bf16[4,1,4,16,192]{4,3,2,0,1:T(8,128)(2,1)S(1)}, u32[]{:S(2)}, u32[]{:S(2)}) collective-permute-start(bf16[4,1,4,16,192]{4,3,2,0,1:T(8,128)(2,1)S(1)} %pad_maximum_fusion.4), channel_id=1, source_target_pairs={{0,7},{1,0},{2,1},{3,2},{4,3},{5,4},{6,5},{7,6},{8,15},{9,8},{10,9... | collective-permute-start | bytes 294920 | tf_op jit(solution)/shard_map/ppermute | solution.py:18
  9.6 4.1 %collective-permute-start.9 = (bf16[2,1,16,16,192]{4,3,2,0,1:T(8,128)(2,1)S(1)}, bf16[2,1,16,16,192]{4,3,2,0,1:T(8,128)(2,1)S(1)}, u32[]{:S(2)}, u32[]{:S(2)}) collective-permute-start(bf16[2,1,16,16,192]{4,3,2,0,1:T(8,128)(2,1)S(1)} %slice.392), channel_id=1, source_target_pairs={{0,8},{8,16},{16,24},{1,9},{9,17},{17,25},{2,10},{10,18},{18,26},{... | collective-permute-start | bytes 589832 | tf_op jit(solution)/shard_map/ppermute | solution.py:26
  13.7 0.7 fusion.71
  14.6 8.1 %collective-permute-done.1 = bf16[4,1,4,16,192]{4,3,2,0,1:T(8,128)(2,1)S(1)} collective-permute-done((bf16[4,1,4,16,192]{4,3,2,0,1:T(8,128)(2,1)S(1)}, bf16[4,1,4,16,192]{4,3,2,0,1:T(8,128)(2,1)S(1)}, u32[]{:S(2)}, u32[]{:S(2)}) %collective-permute-start.1) | collective-permute-done | bytes 98336 | tf_op jit(solution)/shard_map/ppermute | solution.py:16
  22.7 4.2 %collective-permute-start.5 = (bf16[4,1,4,16,192]{4,3,2,0,1:T(8,128)(2,1)S(1)}, bf16[4,1,4,16,192]{4,3,2,0,1:T(8,128)(2,1)S(1)}, u32[]{:S(2)}, u32[]{:S(2)}) collective-permute-start(bf16[4,1,4,16,192]{4,3,2,0,1:T(8,128)(2,1)S(1)} %collective-permute-done.4), channel_id=1, source_target_pairs={{0,7},{1,0},{2,1},{3,2},{4,3},{5,4},{6,5},{7,6},{8,15},{9,8},{10,9... | collective-permute-start | bytes 294920 | tf_op jit(solution)/shard_map/ppermute | solution.py:18
  26.9 3.1 %collective-permute-done.2 = bf16[4,1,4,16,192]{4,3,2,0,1:T(8,128)(2,1)S(1)} collective-permute-done((bf16[4,1,4,16,192]{4,3,2,0,1:T(8,128)(2,1)S(1)}, bf16[4,1,4,16,192]{4,3,2,0,1:T(8,128)(2,1)S(1)}, u32[]{:S(2)}, u32[]{:S(2)}) %collective-permute-start.2) | collective-permute-done | bytes 98336 | tf_op jit(solution)/shard_map/ppermute | solution.py:16
  30.1 4.1 %collective-permute-start.6 = (bf16[4,1,4,16,192]{4,3,2,0,1:T(8,128)(2,1)S(1)}, bf16[4,1,4,16,192]{4,3,2,0,1:T(8,128)(2,1)S(1)}, u32[]{:S(2)}, u32[]{:S(2)}) collective-permute-start(bf16[4,1,4,16,192]{4,3,2,0,1:T(8,128)(2,1)S(1)} %collective-permute-done.5), channel_id=1, source_target_pairs={{0,7},{1,0},{2,1},{3,2},{4,3},{5,4},{6,5},{7,6},{8,15},{9,8},{10,9... | collective-permute-start | bytes 294920 | tf_op jit(solution)/shard_map/ppermute | solution.py:18
  34.2 2.4 %collective-permute-done.3 = bf16[4,1,4,16,192]{4,3,2,0,1:T(8,128)(2,1)S(1)} collective-permute-done((bf16[4,1,4,16,192]{4,3,2,0,1:T(8,128)(2,1)S(1)}, bf16[4,1,4,16,192]{4,3,2,0,1:T(8,128)(2,1)S(1)}, u32[]{:S(2)}, u32[]{:S(2)}) %collective-permute-start.3) | collective-permute-done | bytes 98336 | tf_op jit(solution)/shard_map/ppermute | solution.py:16
  37.7 3.4 %collective-permute-start.7 = (bf16[2,1,4,192]{3,2,0,1:T(4,128)(2,1)S(1)}, bf16[2,1,4,192]{3,2,0,1:T(4,128)(2,1)S(1)}, u32[]{:S(2)}, u32[]{:S(2)}) collective-permute-start(bf16[2,1,4,192]{3,2,0,1:T(4,128)(2,1)S(1)} %slice.382), channel_id=1, source_target_pairs={{0,8},{8,16},{16,24},{1,9},{9,17},{17,25},{2,10},{10,18},{18,26},{... | collective-permute-start | bytes 9224 | tf_op jit(solution)/shard_map/ppermute | solution.py:26
  41.1 0.7 fusion.14
  41.9 1.9 %collective-permute-start.8 = (bf16[2,1,4,16,192]{4,3,0,2,1:T(8,128)(2,1)S(1)}, bf16[2,1,4,16,192]{4,3,0,2,1:T(8,128)(2,1)S(1)}, u32[]{:S(2)}, u32[]{:S(2)}) collective-permute-start(bf16[2,1,4,16,192]{4,3,0,2,1:T(8,128)(2,1)S(1)} %slice.385), channel_id=1, source_target_pairs={{0,8},{8,16},{16,24},{1,9},{9,17},{17,25},{2,10},{10,18},{18,26},{... | collective-permute-start | bytes 147464 | tf_op jit(solution)/shard_map/ppermute | solution.py:26
  43.9 1.3 collective-permute-done.8
  45.5 0.9 pad_maximum_fusion.2
  46.4 24.9 %conditional.2 = (bf16[4,16,16,192]{3,2,1,0:T(8,128)(2,1)S(1)}) conditional(s32[]{:T(128)} %convert_element_type.107, () %tuple.21, (bf16[6,1,18,18,192]{4,3,2,0,1:T(8,128)(2,1)S(1)}, bf16[9,576,192]{1,2,0:T(8,128)(2,1)}, f32[192]{0:T(256)S(1)}, s32[]{:T(128)}, s32[4]{0:T(128)S(1)}, /*index=5*/f32[192]{0:T(256)S(1)}) %tuple.101), branch_computations={%region_1.3_spmd, %region_2.5_spmd} | conditional | flops 2048533504 | bytes 96561936 | solution.py:130
  47.3 0.9 pad_maximum_fusion
  48.1 4.4 %fusion.74 = (bf16[4,16,16,576]{3,2,1,0:T(8,128)(2,1)}, bf16[4,16,16,576]{3,2,1,0:T(8,128)(2,1)}, bf16[4,16,16,576]{3,2,1,0:T(8,128)(2,1)}, bf16[4,16,16,576]{3,...) fusion(bf16[6,18,16,576]{3,2,1,0:T(8,128)(2,1)S(1)} %pad_maximu, ...), kind=kLoop, calls=%fused_computation.197 | loop fusion | bytes 21233664 | tf_op jit(solution)/shard_map/cond/branch_1_fun/slice | solution.py:44
  52.5 4.1 %copy.153 = bf16[9,576,192]{2,1,0:T(8,128)(2,1)S(1)} copy(bf16[9,576,192]{1,2,0:T(8,128)(2,1)} %get-tuple-element.156) | data formatting | bytes 3981312 | tf_op jit(solution)/shard_map
  56.6 2.0 %fusion = f32[1024,192]{0,1:T(8,128)S(1)} fusion(bf16[1024,576]{1,0:T(8,128)(2,1)} %bitcast.249, bf16[9,576,192]{2,1,0:T(8,128)(2,1)S(1)} %copy.153), kind=kOutput, calls=%fused_computation.20 | convolution fusion | flops 226492416 | bytes 2260992 | tf_op jit(solution)/shard_map/cond/branch_1_fun/dot_general | solution.py:47
  61.9 0.7 copy-done.7
  63.2 0.7 copy-done.5
  65.9 0.7 copy-done.1
  66.6 1.5 %convolution_add_fusion.1 = f32[1024,192]{0,1:T(8,128)} fusion(f32[1024,192]{0,1:T(8,128)S(1)} %convolution_add_fusion.2, bf16[1024,576]{1,0:T(8,128)(2,1)S(1)} %bitcast.235, bf16[9,576,192]{2,1,0:T(8,128)(2,1)S(1)} %copy.153), kind=kOutput, calls=%fused_computation.2 | convolution fusion | flops 226689024 | bytes 3178496 | tf_op jit(solution)/shard_map/cond/branch_1_fun/dot_general | solution.py:47
  68.2 2.2 %multiply_reduce_fusion = (f32[1024]{0:T(1024)S(1)}, f32[1024,192]{0,1:T(8,128)S(1)}) fusion(f32[1024]{0:T(1024)S(1)} %mul.124, f32[192]{0:T(256)S(1)} %get-tuple-element.61, f32[1024,192]{0,1:T(8,128)} %convolution_add_fusion.1, bf16[1024,576]{1,0:T(8,128)(2,1)} %bitcast.233, bf16[9,576,192]{2,1,0:T(8,128)(2,1)S(1)} %copy.153), kind=kOutput, calls=%fused_computation.10 | convolution fusion | flops 227474432 | bytes 3056640 | tf_op jit(solution)/shard_map/cond/branch_1_fun/dot_general | solution.py:47
  71.4 1.0 collective-permute-start.10
  72.5 7.0 %collective-permute-done.10 = bf16[4,1,4,16,192]{4,3,2,0,1:T(8,128)(2,1)S(1)} collective-permute-done((bf16[4,1,4,16,192]{4,3,2,0,1:T(8,128)(2,1)S(1)}, bf16[4,1,4,16,192]{4,3,2,0,1:T(8,128)(2,1)S(1)}, u32[]{:S(2)}, u32[]{:S(2)}) %collective-permute-start.10) | collective-permute-done | bytes 98336 | tf_op jit(solution)/shard_map/ppermute | solution.py:16
  79.5 4.2 %collective-permute-start.14 = (bf16[4,1,4,16,192]{4,3,2,0,1:T(8,128)(2,1)S(1)}, bf16[4,1,4,16,192]{4,3,2,0,1:T(8,128)(2,1)S(1)}, u32[]{:S(2)}, u32[]{:S(2)}) collective-permute-start(bf16[4,1,4,16,192]{4,3,2,0,1:T(8,128)(2,1)S(1)} %pad_maximum_fusion.5), channel_id=1, source_target_pairs={{0,7},{1,0},{2,1},{3,2},{4,3},{5,4},{6,5},{7,6},{8,15},{9,8},{10,9... | collective-permute-start | bytes 294920 | tf_op jit(solution)/shard_map/ppermute | solution.py:18
  83.7 2.8 %collective-permute-done.11 = bf16[4,1,4,16,192]{4,3,2,0,1:T(8,128)(2,1)S(1)} collective-permute-done((bf16[4,1,4,16,192]{4,3,2,0,1:T(8,128)(2,1)S(1)}, bf16[4,1,4,16,192]{4,3,2,0,1:T(8,128)(2,1)S(1)}, u32[]{:S(2)}, u32[]{:S(2)}) %collective-permute-start.11) | collective-permute-done | bytes 98336 | tf_op jit(solution)/shard_map/ppermute | solution.py:16
  86.9 3.8 %collective-permute-start.15 = (bf16[4,1,4,16,192]{4,3,2,0,1:T(8,128)(2,1)S(1)}, bf16[4,1,4,16,192]{4,3,2,0,1:T(8,128)(2,1)S(1)}, u32[]{:S(2)}, u32[]{:S(2)}) collective-permute-start(bf16[4,1,4,16,192]{4,3,2,0,1:T(8,128)(2,1)S(1)} %collective-permute-done.14), channel_id=1, source_target_pairs={{0,7},{1,0},{2,1},{3,2},{4,3},{5,4},{6,5},{7,6},{8,15},{9,8},{10,9... | collective-permute-start | bytes 294920 | tf_op jit(solution)/shard_map/ppermute | solution.py:18
  90.6 2.4 %collective-permute-done.12 = bf16[4,1,4,16,192]{4,3,2,0,1:T(8,128)(2,1)S(1)} collective-permute-done((bf16[4,1,4,16,192]{4,3,2,0,1:T(8,128)(2,1)S(1)}, bf16[4,1,4,16,192]{4,3,2,0,1:T(8,128)(2,1)S(1)}, u32[]{:S(2)}, u32[]{:S(2)}) %collective-permute-start.12) | collective-permute-done | bytes 98336 | tf_op jit(solution)/shard_map/ppermute | solution.py:16
  93.1 1.1 collective-permute-start.13
  94.2 5.4 %collective-permute-start.19 = (bf16[2,1,16,16,192]{4,3,2,0,1:T(8,128)(2,1)S(1)}, bf16[2,1,16,16,192]{4,3,2,0,1:T(8,128)(2,1)S(1)}, u32[]{:S(2)}, u32[]{:S(2)}) collective-permute-start(bf16[2,1,16,16,192]{4,3,2,0,1:T(8,128)(2,1)S(1)} %slice_bitcast_fusion.36), channel_id=1, source_target_pairs={{0,8},{8,16},{16,24},{1,9},{9,17},{17,25},{2,10},{10,18},{18,26},{... | collective-permute-start | bytes 589832 | tf_op jit(solution)/shard_map/ppermute | solution.py:26
  99.6 4.5 %collective-permute-start.16 = (bf16[4,1,4,16,192]{4,3,2,0,1:T(8,128)(2,1)S(1)}, bf16[4,1,4,16,192]{4,3,2,0,1:T(8,128)(2,1)S(1)}, u32[]{:S(2)}, u32[]{:S(2)}) collective-permute-start(bf16[4,1,4,16,192]{4,3,2,0,1:T(8,128)(2,1)S(1)} %collective-permute-done.15), channel_id=1, source_target_pairs={{0,7},{1,0},{2,1},{3,2},{4,3},{5,4},{6,5},{7,6},{8,15},{9,8},{10,9... | collective-permute-start | bytes 294920 | tf_op jit(solution)/shard_map/ppermute | solution.py:18
  104.2 1.8 %collective-permute-done.16 = bf16[4,1,4,16,192]{4,3,2,0,1:T(8,128)(2,1)S(1)} collective-permute-done((bf16[4,1,4,16,192]{4,3,2,0,1:T(8,128)(2,1)S(1)}, bf16[4,1,4,16,192]{4,3,2,0,1:T(8,128)(2,1)S(1)}, u32[]{:S(2)}, u32[]{:S(2)}) %collective-permute-start.16) | collective-permute-done | bytes 98336 | tf_op jit(solution)/shard_map/ppermute | solution.py:18
  106.9 2.8 %collective-permute-start.17 = (bf16[2,1,4,192]{3,2,0,1:T(4,128)(2,1)S(1)}, bf16[2,1,4,192]{3,2,0,1:T(4,128)(2,1)S(1)}, u32[]{:S(2)}, u32[]{:S(2)}) collective-permute-start(bf16[2,1,4,192]{3,2,0,1:T(4,128)(2,1)S(1)} %slice.405), channel_id=1, source_target_pairs={{0,8},{8,16},{16,24},{1,9},{9,17},{17,25},{2,10},{10,18},{18,26},{... | collective-permute-start | bytes 9224 | tf_op jit(solution)/shard_map/ppermute | solution.py:26
  109.7 0.7 fusion.12
  110.5 1.9 %collective-permute-start.18 = (bf16[2,1,4,16,192]{4,3,0,2,1:T(8,128)(2,1)S(1)}, bf16[2,1,4,16,192]{4,3,0,2,1:T(8,128)(2,1)S(1)}, u32[]{:S(2)}, u32[]{:S(2)}) collective-permute-start(bf16[2,1,4,16,192]{4,3,0,2,1:T(8,128)(2,1)S(1)} %slice.408), channel_id=1, source_target_pairs={{0,8},{8,16},{16,24},{1,9},{9,17},{17,25},{2,10},{10,18},{18,26},{... | collective-permute-start | bytes 147464 | tf_op jit(solution)/shard_map/ppermute | solution.py:26
  112.4 1.3 collective-permute-done.18
  114.0 0.9 pad_maximum_fusion.3
  114.9 24.5 %conditional.3 = (bf16[4,1,16,3072]{3,2,0,1:T(8,128)(2,1)}) conditional(s32[]{:T(128)} %convert_element_type.107, () %tuple.20, (bf16[6,1,18,18,192]{4,3,2,0,1:T(8,128)(2,1)S(1)}, bf16[9,576,192]{1,2,0:T(8,128)(2,1)}, f32[192]{0:T(256)S(1)}, s32[]{:T(128)}, s32[4]{0:T(128)S(1)}, /*index=5*/bf16[4]{0:T(256)(128)(2,1)S(1)}, ...), branch_computations={%region_4.6_spmd, %region_5.7_spmd} | conditional | flops 2047156224 | bytes 104957008 | solution.py:130
  115.8 0.9 pad_maximum_fusion.1
  116.7 4.4 %fusion.76 = (bf16[4,16,16,576]{3,2,1,0:T(8,128)(2,1)}, bf16[4,16,16,576]{3,2,1,0:T(8,128)(2,1)}, bf16[4,16,16,576]{3,2,1,0:T(8,128)(2,1)}, bf16[4,16,16,576]{3,...) fusion(bf16[6,18,16,576]{3,2,1,0:T(8,128)(2,1)S(1)} %pad_maximu, ...), kind=kLoop, calls=%fused_computation.199 | loop fusion | bytes 21233664 | tf_op jit(solution)/shard_map/cond/branch_1_fun/slice | solution.py:44
  121.1 4.1 %copy.164 = bf16[9,576,192]{2,1,0:T(8,128)(2,1)S(1)} copy(bf16[9,576,192]{1,2,0:T(8,128)(2,1)} %get-tuple-element.162) | data formatting | bytes 3981312 | tf_op jit(solution)/shard_map
  125.2 2.0 %fusion.1 = f32[1024,192]{0,1:T(8,128)S(1)} fusion(bf16[1024,576]{1,0:T(8,128)(2,1)} %bitcast.250, bf16[9,576,192]{2,1,0:T(8,128)(2,1)S(1)} %copy.164), kind=kOutput, calls=%fused_computation.43 | convolution fusion | flops 226492416 | bytes 2260992 | tf_op jit(solution)/shard_map/cond/branch_1_fun/dot_general | solution.py:47
  130.5 0.7 copy-done.8
  138.4 0.9 add_convert_fusion
  (151 shorter events, 22.6 us)
Async XLA Ops:
  0.0 3.7 %copy-start.17 = (f32[192]{0:T(256)S(1)}, f32[192]{0:T(256)}, u32[]{:S(2)}) copy-start(f32[192]{0:T(256)} %param.18) | copy-start | bytes 2308
  4.3 10.1 %collective-permute-start = (bf16[4,1,4,16,192]{4,3,2,0,1:T(8,128)(2,1)S(1)}, bf16[4,1,4,16,192]{4,3,2,0,1:T(8,128)(2,1)S(1)}, u32[]{:S(2)}, u32[]{:S(2)}) collective-permute-start(bf16[4,1,4,16,192]{4,3,2,0,1:T(8,128)(2,1)S(1)} %pad_maximum_fusion.4), channel_id=1, source_target_pairs={{0,1},{1,2},{2,3},{3,4},{4,5},{5,6},{6,7},{7,0},{8,9},{9,10},{10,1... | collective-permute-start | bytes 294920 | tf_op jit(solution)/shard_map/ppermute | solution.py:16
  6.5 16.3 %collective-permute-start.4 = (bf16[4,1,4,16,192]{4,3,2,0,1:T(8,128)(2,1)S(1)}, bf16[4,1,4,16,192]{4,3,2,0,1:T(8,128)(2,1)S(1)}, u32[]{:S(2)}, u32[]{:S(2)}) collective-permute-start(bf16[4,1,4,16,192]{4,3,2,0,1:T(8,128)(2,1)S(1)} %pad_maximum_fusion.4), channel_id=1, source_target_pairs={{0,7},{1,0},{2,1},{3,2},{4,3},{5,4},{6,5},{7,6},{8,15},{9,8},{10,9... | collective-permute-start | bytes 294920 | tf_op jit(solution)/shard_map/ppermute | solution.py:18
  9.6 35.9 %collective-permute-start.9 = (bf16[2,1,16,16,192]{4,3,2,0,1:T(8,128)(2,1)S(1)}, bf16[2,1,16,16,192]{4,3,2,0,1:T(8,128)(2,1)S(1)}, u32[]{:S(2)}, u32[]{:S(2)}) collective-permute-start(bf16[2,1,16,16,192]{4,3,2,0,1:T(8,128)(2,1)S(1)} %slice.392), channel_id=1, source_target_pairs={{0,8},{8,16},{16,24},{1,9},{9,17},{17,25},{2,10},{10,18},{18,26},{... | collective-permute-start | bytes 589832 | tf_op jit(solution)/shard_map/ppermute | solution.py:26
  14.5 8.2 %collective-permute-start.1 = (bf16[4,1,4,16,192]{4,3,2,0,1:T(8,128)(2,1)S(1)}, bf16[4,1,4,16,192]{4,3,2,0,1:T(8,128)(2,1)S(1)}, u32[]{:S(2)}, u32[]{:S(2)}) collective-permute-start(bf16[4,1,4,16,192]{4,3,2,0,1:T(8,128)(2,1)S(1)} %collective-permute-done), channel_id=1, source_target_pairs={{0,1},{1,2},{2,3},{3,4},{4,5},{5,6},{6,7},{7,0},{8,9},{9,10},{10,1... | collective-permute-start | bytes 294920 | tf_op jit(solution)/shard_map/ppermute | solution.py:16
  22.7 7.4 %collective-permute-start.2 = (bf16[4,1,4,16,192]{4,3,2,0,1:T(8,128)(2,1)S(1)}, bf16[4,1,4,16,192]{4,3,2,0,1:T(8,128)(2,1)S(1)}, u32[]{:S(2)}, u32[]{:S(2)}) collective-permute-start(bf16[4,1,4,16,192]{4,3,2,0,1:T(8,128)(2,1)S(1)} %collective-permute-done.1), channel_id=1, source_target_pairs={{0,1},{1,2},{2,3},{3,4},{4,5},{5,6},{6,7},{7,0},{8,9},{9,10},{10,1... | collective-permute-start | bytes 294920 | tf_op jit(solution)/shard_map/ppermute | solution.py:16
  22.7 7.4 %collective-permute-start.5 = (bf16[4,1,4,16,192]{4,3,2,0,1:T(8,128)(2,1)S(1)}, bf16[4,1,4,16,192]{4,3,2,0,1:T(8,128)(2,1)S(1)}, u32[]{:S(2)}, u32[]{:S(2)}) collective-permute-start(bf16[4,1,4,16,192]{4,3,2,0,1:T(8,128)(2,1)S(1)} %collective-permute-done.4), channel_id=1, source_target_pairs={{0,7},{1,0},{2,1},{3,2},{4,3},{5,4},{6,5},{7,6},{8,15},{9,8},{10,9... | collective-permute-start | bytes 294920 | tf_op jit(solution)/shard_map/ppermute | solution.py:18
  30.1 6.6 %collective-permute-start.3 = (bf16[4,1,4,16,192]{4,3,2,0,1:T(8,128)(2,1)S(1)}, bf16[4,1,4,16,192]{4,3,2,0,1:T(8,128)(2,1)S(1)}, u32[]{:S(2)}, u32[]{:S(2)}) collective-permute-start(bf16[4,1,4,16,192]{4,3,2,0,1:T(8,128)(2,1)S(1)} %collective-permute-done.2), channel_id=1, source_target_pairs={{0,1},{1,2},{2,3},{3,4},{4,5},{5,6},{6,7},{7,0},{8,9},{9,10},{10,1... | collective-permute-start | bytes 294920 | tf_op jit(solution)/shard_map/ppermute | solution.py:16
  30.1 6.7 %collective-permute-start.6 = (bf16[4,1,4,16,192]{4,3,2,0,1:T(8,128)(2,1)S(1)}, bf16[4,1,4,16,192]{4,3,2,0,1:T(8,128)(2,1)S(1)}, u32[]{:S(2)}, u32[]{:S(2)}) collective-permute-start(bf16[4,1,4,16,192]{4,3,2,0,1:T(8,128)(2,1)S(1)} %collective-permute-done.5), channel_id=1, source_target_pairs={{0,7},{1,0},{2,1},{3,2},{4,3},{5,4},{6,5},{7,6},{8,15},{9,8},{10,9... | collective-permute-start | bytes 294920 | tf_op jit(solution)/shard_map/ppermute | solution.py:18
  37.7 6.2 %collective-permute-start.7 = (bf16[2,1,4,192]{3,2,0,1:T(4,128)(2,1)S(1)}, bf16[2,1,4,192]{3,2,0,1:T(4,128)(2,1)S(1)}, u32[]{:S(2)}, u32[]{:S(2)}) collective-permute-start(bf16[2,1,4,192]{3,2,0,1:T(4,128)(2,1)S(1)} %slice.382), channel_id=1, source_target_pairs={{0,8},{8,16},{16,24},{1,9},{9,17},{17,25},{2,10},{10,18},{18,26},{... | collective-permute-start | bytes 9224 | tf_op jit(solution)/shard_map/ppermute | solution.py:26
  41.9 3.2 %collective-permute-start.8 = (bf16[2,1,4,16,192]{4,3,0,2,1:T(8,128)(2,1)S(1)}, bf16[2,1,4,16,192]{4,3,0,2,1:T(8,128)(2,1)S(1)}, u32[]{:S(2)}, u32[]{:S(2)}) collective-permute-start(bf16[2,1,4,16,192]{4,3,0,2,1:T(8,128)(2,1)S(1)} %slice.385), channel_id=1, source_target_pairs={{0,8},{8,16},{16,24},{1,9},{9,17},{17,25},{2,10},{10,18},{18,26},{... | collective-permute-start | bytes 147464 | tf_op jit(solution)/shard_map/ppermute | solution.py:26
  45.4 1.0 copy-start.16
  45.4 1.0 copy-start.19
  56.6 2.0 %copy-start.13 = (bf16[4,16,16,576]{3,2,1,0:T(8,128)(2,1)S(1)}, bf16[4,16,16,576]{3,2,1,0:T(8,128)(2,1)}, u32[]{:S(2)}) copy-start(bf16[4,16,16,576]{3,2,1,0:T(8,128)(2,1)} %get-tuple-element.175) | copy-start | bytes 3538948 | tf_op jit(solution)/shard_map/cond
  58.7 1.3 copy-start.11
  60.0 1.3 copy-start.9
  61.3 1.3 copy-start.7
  62.6 1.3 copy-start.5
  63.9 1.3 copy-start.3
  65.2 1.3 copy-start.1
  71.4 8.1 %collective-permute-start.10 = (bf16[4,1,4,16,192]{4,3,2,0,1:T(8,128)(2,1)S(1)}, bf16[4,1,4,16,192]{4,3,2,0,1:T(8,128)(2,1)S(1)}, u32[]{:S(2)}, u32[]{:S(2)}) collective-permute-start(bf16[4,1,4,16,192]{4,3,2,0,1:T(8,128)(2,1)S(1)} %pad_maximum_fusion.5), channel_id=1, source_target_pairs={{0,1},{1,2},{2,3},{3,4},{4,5},{5,6},{6,7},{7,0},{8,9},{9,10},{10,1... | collective-permute-start | bytes 294920 | tf_op jit(solution)/shard_map/ppermute | solution.py:16
  79.5 7.0 %collective-permute-start.11 = (bf16[4,1,4,16,192]{4,3,2,0,1:T(8,128)(2,1)S(1)}, bf16[4,1,4,16,192]{4,3,2,0,1:T(8,128)(2,1)S(1)}, u32[]{:S(2)}, u32[]{:S(2)}) collective-permute-start(bf16[4,1,4,16,192]{4,3,2,0,1:T(8,128)(2,1)S(1)} %collective-permute-done.10), channel_id=1, source_target_pairs={{0,1},{1,2},{2,3},{3,4},{4,5},{5,6},{6,7},{7,0},{8,9},{9,10},{10,1... | collective-permute-start | bytes 294920 | tf_op jit(solution)/shard_map/ppermute | solution.py:16
  79.5 7.4 %collective-permute-start.14 = (bf16[4,1,4,16,192]{4,3,2,0,1:T(8,128)(2,1)S(1)}, bf16[4,1,4,16,192]{4,3,2,0,1:T(8,128)(2,1)S(1)}, u32[]{:S(2)}, u32[]{:S(2)}) collective-permute-start(bf16[4,1,4,16,192]{4,3,2,0,1:T(8,128)(2,1)S(1)} %pad_maximum_fusion.5), channel_id=1, source_target_pairs={{0,7},{1,0},{2,1},{3,2},{4,3},{5,4},{6,5},{7,6},{8,15},{9,8},{10,9... | collective-permute-start | bytes 294920 | tf_op jit(solution)/shard_map/ppermute | solution.py:18
  86.5 6.6 %collective-permute-start.12 = (bf16[4,1,4,16,192]{4,3,2,0,1:T(8,128)(2,1)S(1)}, bf16[4,1,4,16,192]{4,3,2,0,1:T(8,128)(2,1)S(1)}, u32[]{:S(2)}, u32[]{:S(2)}) collective-permute-start(bf16[4,1,4,16,192]{4,3,2,0,1:T(8,128)(2,1)S(1)} %collective-permute-done.11), channel_id=1, source_target_pairs={{0,1},{1,2},{2,3},{3,4},{4,5},{5,6},{6,7},{7,0},{8,9},{9,10},{10,1... | collective-permute-start | bytes 294920 | tf_op jit(solution)/shard_map/ppermute | solution.py:16
  86.9 12.7 %collective-permute-start.15 = (bf16[4,1,4,16,192]{4,3,2,0,1:T(8,128)(2,1)S(1)}, bf16[4,1,4,16,192]{4,3,2,0,1:T(8,128)(2,1)S(1)}, u32[]{:S(2)}, u32[]{:S(2)}) collective-permute-start(bf16[4,1,4,16,192]{4,3,2,0,1:T(8,128)(2,1)S(1)} %collective-permute-done.14), channel_id=1, source_target_pairs={{0,7},{1,0},{2,1},{3,2},{4,3},{5,4},{6,5},{7,6},{8,15},{9,8},{10,9... | collective-permute-start | bytes 294920 | tf_op jit(solution)/shard_map/ppermute | solution.py:18
  93.1 11.0 %collective-permute-start.13 = (bf16[4,1,4,16,192]{4,3,2,0,1:T(8,128)(2,1)S(1)}, bf16[4,1,4,16,192]{4,3,2,0,1:T(8,128)(2,1)S(1)}, u32[]{:S(2)}, u32[]{:S(2)}) collective-permute-start(bf16[4,1,4,16,192]{4,3,2,0,1:T(8,128)(2,1)S(1)} %collective-permute-done.12), channel_id=1, source_target_pairs={{0,1},{1,2},{2,3},{3,4},{4,5},{5,6},{6,7},{7,0},{8,9},{9,10},{10,1... | collective-permute-start | bytes 294920 | tf_op jit(solution)/shard_map/ppermute | solution.py:16
  94.2 19.8 %collective-permute-start.19 = (bf16[2,1,16,16,192]{4,3,2,0,1:T(8,128)(2,1)S(1)}, bf16[2,1,16,16,192]{4,3,2,0,1:T(8,128)(2,1)S(1)}, u32[]{:S(2)}, u32[]{:S(2)}) collective-permute-start(bf16[2,1,16,16,192]{4,3,2,0,1:T(8,128)(2,1)S(1)} %slice_bitcast_fusion.36), channel_id=1, source_target_pairs={{0,8},{8,16},{16,24},{1,9},{9,17},{17,25},{2,10},{10,18},{18,26},{... | collective-permute-start | bytes 589832 | tf_op jit(solution)/shard_map/ppermute | solution.py:26
  99.6 6.4 %collective-permute-start.16 = (bf16[4,1,4,16,192]{4,3,2,0,1:T(8,128)(2,1)S(1)}, bf16[4,1,4,16,192]{4,3,2,0,1:T(8,128)(2,1)S(1)}, u32[]{:S(2)}, u32[]{:S(2)}) collective-permute-start(bf16[4,1,4,16,192]{4,3,2,0,1:T(8,128)(2,1)S(1)} %collective-permute-done.15), channel_id=1, source_target_pairs={{0,7},{1,0},{2,1},{3,2},{4,3},{5,4},{6,5},{7,6},{8,15},{9,8},{10,9... | collective-permute-start | bytes 294920 | tf_op jit(solution)/shard_map/ppermute | solution.py:18
  106.9 5.5 %collective-permute-start.17 = (bf16[2,1,4,192]{3,2,0,1:T(4,128)(2,1)S(1)}, bf16[2,1,4,192]{3,2,0,1:T(4,128)(2,1)S(1)}, u32[]{:S(2)}, u32[]{:S(2)}) collective-permute-start(bf16[2,1,4,192]{3,2,0,1:T(4,128)(2,1)S(1)} %slice.405), channel_id=1, source_target_pairs={{0,8},{8,16},{16,24},{1,9},{9,17},{17,25},{2,10},{10,18},{18,26},{... | collective-permute-start | bytes 9224 | tf_op jit(solution)/shard_map/ppermute | solution.py:26
  110.5 3.2 %collective-permute-start.18 = (bf16[2,1,4,16,192]{4,3,0,2,1:T(8,128)(2,1)S(1)}, bf16[2,1,4,16,192]{4,3,0,2,1:T(8,128)(2,1)S(1)}, u32[]{:S(2)}, u32[]{:S(2)}) collective-permute-start(bf16[2,1,4,16,192]{4,3,0,2,1:T(8,128)(2,1)S(1)} %slice.408), channel_id=1, source_target_pairs={{0,8},{8,16},{16,24},{1,9},{9,17},{17,25},{2,10},{10,18},{18,26},{... | collective-permute-start | bytes 147464 | tf_op jit(solution)/shard_map/ppermute | solution.py:26
  113.9 0.9 copy-start.18
  125.2 2.0 %copy-start.14 = (bf16[4,16,16,576]{3,2,1,0:T(8,128)(2,1)S(1)}, bf16[4,16,16,576]{3,2,1,0:T(8,128)(2,1)}, u32[]{:S(2)}) copy-start(bf16[4,16,16,576]{3,2,1,0:T(8,128)(2,1)} %get-tuple-element.189) | copy-start | bytes 3538948 | tf_op jit(solution)/shard_map/cond
  127.2 1.3 copy-start.12
  128.6 1.3 copy-start.10
  129.9 1.3 copy-start.8
  131.2 1.3 copy-start.6
  132.5 1.3 copy-start.4
  133.8 1.3 copy-start.2
  135.1 1.3 copy-start
  137.4 1.0 copy-start.15
